TPU v7x, 32 devices: a whole 2x2x4 slice. The times are simulated.
32 devices in a mesh: req: 2 (over x), ctx: 4 (over y, core), tp: 4 (over z).
Axes of the slice: x: 2, y: 2, z: 4, core: 2. Of those that a mesh axis runs over, the one named last changes fastest.
Arguments:
- queries: bfloat16 [512, 16, 128], P('req', 'tp'), may hold values from -5 to 5
- new_keys: bfloat16 [512, 4, 128], P('req', 'tp'), may hold values from -5 to 5
- new_values: bfloat16 [512, 4, 128], P('req', 'tp'), may hold values from -24 to 24
- cache_keys: bfloat16 [2, 8192, 4, 128], P('req', 'ctx', 'tp'), may hold values from -5 to 5
- cache_values: bfloat16 [2, 8192, 4, 128], P('req', 'ctx', 'tp'), may hold values from -24 to 24
- cache_lengths: int32 [2], replicated, may hold values from 1 to 8192, as said below
- residual: bfloat16 [512, 2048], P(('req', 'ctx'), 'tp'), may hold values from -24 to 24
- out_weight: bfloat16 [2048, 2048], P('tp', 'ctx'), may hold values from -0.52734375 to 0.52734375
- norm_gain: float32 [2048], replicated, may hold values from 0.1 to 1.9
- expert_ids: int32 [512, 6], P(('req', 'ctx')), may hold values from 0 to 63, all different within a row; in each aligned block of 64 rows (0 to 63, 64 to 127, ...) at most 8 rows name the same one
- gate_weights: float32 [512, 6], P(('req', 'ctx')), may hold values from 0.1 to 1
- w_gate: bfloat16 [64, 2048, 1408], P('req', 'ctx', 'tp'), may hold values from -0.125 to 0.125
- w_up: bfloat16 [64, 2048, 1408], P('req', 'ctx', 'tp'), may hold values from -0.125 to 0.125
- w_down: bfloat16 [64, 1408, 2048], P('req', 'tp', 'ctx'), may hold values from -0.15625 to 0.15625
Outputs:
- layer_out: bfloat16 [512, 2048], P(('req', 'ctx'), 'tp')
Inputs may be any that keep to these rules, and one draw needn't show every extreme that they name: `cache_lengths`: the longest cached length equals 8192. `expert_ids`: within each aligned block of 64 tokens no expert is named by more than 8 routes, a bound that some block reaches.
All inputs are finite; a program needn't handle non-finite values.
Results may differ from a plain program's by a relative error of at most 0.006.
Values may be sent and summed in bfloat16 or wider, within the bound.
A program may use at most 384 MiB of HBM per device.

v0:
```python
import jax
import jax.numpy as jnp
from jax import lax
from jax.sharding import PartitionSpec as P

HD = 128
TOP = 6
CAP = 8


masked_score = -1e30


def merged_2(value, axis, join):
    pieces = jax.tree.map(lambda part: lax.all_gather(part, axis), value)
    head = jax.tree.map(lambda part: part[0], pieces)
    tail = jax.tree.map(lambda part: part[1:], pieces)
    so_far, _ = lax.scan(lambda so_far, piece: (join(so_far, piece), None), head, tail)
    return so_far


def joined_outputs(left_part, right_portion):
    highest = jnp.maximum(left_part[0], right_portion[0])
    left_factor = jnp.exp(left_part[0] - highest)
    right_factor = jnp.exp(right_portion[0] - highest)
    totals = left_part[1] * left_factor + right_portion[1] * right_factor
    numerator = left_part[2] * left_factor[..., None] + right_portion[2] * right_factor[..., None]
    return (highest, totals, numerator)


def body(
    queries,
    new_keys,
    new_values,
    cache_keys,
    cache_values,
    cache_lengths,
    residual,
    out_weight,
    norm_gain,
    expert_ids,
    gate_weights,
    w_gate,
    w_up,
    w_down,
):
    ctx_pos = lax.axis_index("ctx")
    tp_pos = lax.axis_index("tp")
    req_pos = lax.axis_index("req")
    ctx_count = lax.axis_size("ctx")
    tp_count = lax.axis_size("tp")
    req_count = lax.axis_size("req")
    tok_dev, head_count, head_size = queries.shape
    cache_dev = cache_keys.shape[1]
    model_width = w_down.shape[2] * ctx_count
    d_share = residual.shape[1]
    expert_mixture_device = tok_dev // ctx_count
    scale = 1.0 / HD**0.5
    query_flat = queries.reshape(tok_dev * head_count, head_size)
    key_rows = jnp.concatenate([cache_keys[0, :, 0, :], new_keys[:, 0, :]], 0)
    value_rows = jnp.concatenate([cache_values[0, :, 0, :], new_values[:, 0, :]], 0)
    length = lax.dynamic_index_in_dim(cache_lengths, req_pos, 0, keepdims=False)
    cache_valid = ctx_pos * cache_dev + jnp.arange(cache_dev, dtype=jnp.int32) < length
    is_last = ctx_pos == ctx_count - 1
    positions = jnp.arange(tok_dev, dtype=jnp.int32)
    causal = jnp.logical_and(positions[None, :] <= positions[:, None], is_last)
    valid = jnp.concatenate(
        [jnp.broadcast_to(cache_valid[None, :], (tok_dev, cache_dev)), causal], 1
    )
    scores = jnp.dot(query_flat, key_rows.T, preferred_element_type=jnp.float32) * scale
    scores = scores.reshape(tok_dev, head_count, cache_dev + tok_dev)
    scores = jnp.where(valid[:, None, :], scores, masked_score)
    local_max = jnp.max(scores, -1)
    probabilities = jnp.where(valid[:, None, :], jnp.exp(scores - local_max[..., None]), 0.0)
    local_sum = jnp.sum(probabilities, -1)
    rounded = probabilities.astype(jnp.bfloat16)
    numerator = jnp.einsum("thk,kd->thd", rounded, value_rows, preferred_element_type=jnp.float32)
    row_start = ctx_pos * expert_mixture_device
    col_start = tp_pos * d_share
    highest, totals, merged = merged_2((local_max, local_sum, numerator), "ctx", joined_outputs)
    attention_result = merged / totals[..., None]
    attention_result = lax.dynamic_slice_in_dim(
        attention_result, row_start, expert_mixture_device, 0
    )
    attention_result = attention_result.astype(jnp.bfloat16).reshape(
        expert_mixture_device, head_count * head_size
    )
    partial_value = jnp.dot(
        attention_result,
        lax.all_gather(out_weight, "ctx", axis=1, tiled=True),
        preferred_element_type=jnp.float32,
    )
    corner = lax.dynamic_slice_in_dim(partial_value, col_start, d_share, 1) + residual.astype(
        jnp.float32
    )
    partial_value = lax.dynamic_update_slice(partial_value, corner, (jnp.int32(0), col_start))
    hidden = lax.psum(partial_value, "tp")
    mean_square = jnp.mean(hidden * hidden, -1, keepdims=True)
    normed = (hidden * lax.rsqrt(mean_square + 1e-06) * norm_gain).astype(jnp.bfloat16)
    full_gate, full_up, full_down = (
        lax.all_gather(w_gate, "ctx", axis=1, tiled=True),
        lax.all_gather(w_up, "ctx", axis=1, tiled=True),
        lax.all_gather(w_down, "ctx", axis=2, tiled=True),
    )
    exp_dev = w_gate.shape[0]
    experts_all = exp_dev * req_count
    flat_ids = expert_ids.reshape(-1)
    route_count = flat_ids.shape[0]
    matches = (flat_ids[:, None] == jnp.arange(experts_all, dtype=jnp.int32)[None, :]).astype(
        jnp.int32
    )
    rank_in = jnp.sum(jnp.cumsum(matches, 0) * matches, 1) - 1
    slot_index = flat_ids * CAP + rank_in
    source = jnp.arange(route_count, dtype=jnp.int32) // TOP
    outgoing = (
        jnp.zeros((experts_all * CAP, model_width), jnp.bfloat16).at[slot_index].set(normed[source])
    )
    outgoing = outgoing.reshape(req_count, exp_dev, CAP, model_width)
    gathered = lax.all_to_all(outgoing, "req", split_axis=0, concat_axis=0, tiled=True)
    gate_act = jnp.einsum("resd,edf->resf", gathered, full_gate, preferred_element_type=jnp.float32)
    up_act = jnp.einsum("resd,edf->resf", gathered, full_up, preferred_element_type=jnp.float32)
    inner = (jax.nn.silu(gate_act) * up_act).astype(jnp.bfloat16)
    down_act = jnp.einsum("resf,efd->resd", inner, full_down, preferred_element_type=jnp.float32)
    expert_out = down_act.astype(jnp.bfloat16)
    returned_rows = lax.all_to_all(
        lax.all_to_all(expert_out, "req", split_axis=0, concat_axis=0, tiled=True),
        "tp",
        split_axis=3,
        concat_axis=2,
        tiled=True,
    )
    slot_sums = (
        returned_rows.reshape(req_count, exp_dev, tp_count, CAP, d_share).astype(jnp.float32).sum(2)
    )
    slot_sums = slot_sums.reshape(experts_all * CAP, d_share)
    picked = slot_sums[slot_index] * gate_weights.reshape(-1)[:, None]
    expert_mixture = picked.reshape(expert_mixture_device, TOP, d_share).sum(1)
    residual_part = lax.dynamic_slice_in_dim(hidden, col_start, d_share, 1)
    return (residual_part + expert_mixture).astype(jnp.bfloat16)


def solution(mesh):
    in_specs = (
        P("req", "tp", None),
        P("req", "tp", None),
        P("req", "tp", None),
        P("req", "ctx", "tp", None),
        P("req", "ctx", "tp", None),
        P(),
        P(("req", "ctx"), "tp"),
        P("tp", "ctx"),
        P(),
        P(("req", "ctx"), None),
        P(("req", "ctx"), None),
        P("req", "ctx", "tp"),
        P("req", "ctx", "tp"),
        P("req", "tp", "ctx"),
    )
    out_specs = P(("req", "ctx"), "tp")
    return jax.shard_map(body, mesh=mesh, in_specs=in_specs, out_specs=out_specs, check_vma=False)
```

profile of v0, /device:TPU:1, one launch (start us, length us, event | category | flops | bytes accessed | tf_op | source)
XLA Modules:
  0.0 1104.5 jit_solution(16539856928096114020)
XLA Ops:
  12.2 5.6 broadcast_in_dim.49
  17.8 6.7 fusion.14
  24.7 11.4 %reshape.151 = f32[256,4,2304]{2,1,0:T(4,128)} reshape(f32[1024,2304]{1,0:T(8,128)} %get-tuple-element.92) | data formatting | bytes 18874368 | tf_op jit(solution)/shard_map/reshape | solution.py:71
  36.1 8.0 fusion.15
  45.1 5.3 select_reduce_fusion
  50.6 6.1 all_gather.33
  56.8 5.6 all_gather.31
  62.4 7.1 all-gather.15.cloned.1.call-done
  77.3 16.4 %all-gather.7.cloned.1.call-done = bf16[512,2048]{1,0:T(8,128)(2,1)} async-done(((bf16[512,512]{1,0:T(8,128)(2,1)}), bf16[512,2048]{1,0:T(8,128)(2,1)}) %all-gather.7.cloned.1.call-update) | async-done | bytes 2097168 | tf_op jit(solution)/shard_map/all_gather | solution.py:90
  100.5 33.2 %all-reduce.2.cloned.1.call-done = f32[64,2048]{1,0:T(8,128)} async-done(((f32[64,2048]{1,0:T(8,128)}), f32[64,2048]{1,0:T(8,128)}) %all-reduce.2.cloned.1.call-update) | async-done | bytes 524304 | tf_op jit(solution)/shard_map/psum | solution.py:97
  136.1 9.5 scatter_custom_fusion
  145.6 27.5 %all_to_all.19 = bf16[2,32,8,2048]{3,2,1,0:T(8,128)(2,1)S(1)} all-to-all(bf16[2,32,8,2048]{3,2,1,0:T(8,128)(2,1)} %bitcast.108), channel_id=1, replica_groups=mesh['req'=2,'ctx'=4,'tp'=4] {'req'}, dimensions={0} | all-to-all | bytes 4194304 | tf_op jit(solution)/shard_map/all_to_all | solution.py:119
  173.1 237.1 %all-gather.9.cloned.1.call-done = bf16[32,2048,352]{1,2,0:T(8,128)(2,1)} async-done(((bf16[32,512,352]{1,2,0:T(8,128)(2,1)}), bf16[32,2048,352]{1,2,0:T(8,128)(2,1)}) %all-gather.9.cloned.1.call-update) | async-done | bytes 46137360 | tf_op jit(solution)/shard_map/all_gather | solution.py:101
  410.2 24.8 %fusion.28 = f32[2,32,8,352]{3,2,0,1:T(8,128)S(1)} fusion(bf16[32,2048,352]{1,2,0:T(8,128)(2,1)} %all-gather.9.cloned.1.call-done, bf16[2,32,8,2048]{3,2,1,0:T(8,128)(2,1)S(1)} %all_to_all.19), kind=kOutput, calls=%fused_computation.38 | convolution fusion | flops 738197504 | bytes 48955392 | tf_op jit(solution)/shard_map/resd,edf->resf/dot_general | solution.py:120
  434.9 250.3 %all-gather.11.cloned.1.call-done = bf16[32,2048,352]{1,2,0:T(8,128)(2,1)} async-done(((bf16[32,512,352]{1,2,0:T(8,128)(2,1)}), bf16[32,2048,352]{1,2,0:T(8,128)(2,1)}) %all-gather.11.cloned.1.call-update) | async-done | bytes 46137360 | tf_op jit(solution)/shard_map/all_gather | solution.py:102
  685.2 25.0 %fusion.43 = bf16[2,32,8,352]{3,2,0,1:T(8,128)(2,1)S(1)} fusion(bf16[32,2048,352]{1,2,0:T(8,128)(2,1)} %all-gather.11.cloned.1.call-done, bf16[2,32,8,2048]{3,2,1,0:T(8,128)(2,1)S(1)} %all_to_all.19, f32[2,32,8,352]{3,2,0,1:T(8,128)S(1)} %fusion.28), kind=kOutput, calls=%fused_computation.41 | convolution fusion | flops 739278848 | bytes 49315840 | tf_op jit(solution)/shard_map/resd,edf->resf/dot_general | solution.py:121
  710.3 250.0 %all-gather.13.cloned.1.call-done = bf16[32,352,2048]{2,1,0:T(8,128)(2,1)} async-done(((bf16[32,352,512]{2,1,0:T(8,128)(2,1)}), bf16[32,352,2048]{2,1,0:T(8,128)(2,1)}) %all-gather.13.cloned.1.call-update) | async-done | bytes 46137360 | tf_op jit(solution)/shard_map/all_gather | solution.py:103
  960.3 17.5 %fusion.21 = bf16[2,32,8,2048]{3,2,0,1:T(8,128)(2,1)S(1)} fusion(bf16[2,32,8,352]{3,2,0,1:T(8,128)(2,1)S(1)} %fusion.43, bf16[32,352,2048]{2,1,0:T(8,128)(2,1)} %all-gather.13.cloned.1.call-done), kind=kOutput, calls=%fused_computation.32 | convolution fusion | flops 739246080 | bytes 48594944 | tf_op jit(solution)/shard_map/resf,efd->resd/dot_general | solution.py:123
  977.9 27.3 %all_to_all.20 = bf16[2,32,8,2048]{3,2,1,0:T(8,128)(2,1)S(1)} all-to-all(bf16[2,32,8,2048]{3,2,1,0:T(8,128)(2,1)S(1)} %copy.78), channel_id=1, replica_groups=mesh['req'=2,'ctx'=4,'tp'=4] {'req'}, dimensions={0} | all-to-all | bytes 4194304 | tf_op jit(solution)/shard_map/all_to_all | solution.py:126
  1005.2 9.1 copy.79
  1014.2 10.5 reshape.199
  1029.6 47.6 %all-to-all-done.2 = bf16[4,2,131072]{2,1,0:T(2,128)(2,1)S(1)} async-done(((bf16[4,2,131072]{2,1,0:T(2,128)(2,1)}), bf16[4,2,131072]{2,1,0:T(2,128)(2,1)S(1)}, u32[]{:S(2)}, u32[]{:S(2)}) %all-to-all-start.2) | async-done | bytes 2097184 | tf_op jit(solution)/shard_map/all_to_all | solution.py:125
  1077.2 5.6 reshape.200
  1082.8 7.5 convert_reduce_fusion
  (97 shorter events, 40.5 us)
Async XLA Ops:
  6.5 11.3 %copy-start = (bf16[256,4,128]{2,1,0:T(4,128)(2,1)S(1)}, bf16[256,4,128]{2,1,0:T(4,128)(2,1)}, u32[]{:S(2)}) copy-start(bf16[256,4,128]{2,1,0:T(4,128)(2,1)} %param.16) | copy-start | bytes 786436
  6.5 62.9 %all-gather.15.cloned.1.call-start = ((), (), s32[]{:S(2)}) async-start(), calls=%async_computation.8 | async-start | bytes 2621440 | tf_op jit(solution)/shard_map/all_gather | solution.py:15
  12.2 5.6 copy-start.3
  24.7 11.4 %copy-start.8 = (bf16[256,1,128]{2,0,1:T(8,128)(2,1)S(1)}, bf16[256,1,128]{2,0,1:T(8,128)(2,1)}, u32[]{:S(2)}) copy-start(bf16[256,1,128]{2,0,1:T(8,128)(2,1)} %param.18) | copy-start | bytes 196612
  44.1 49.5 %all-gather.7.cloned.1.call-start = ((), (), s32[]{:S(2)}) async-start(), calls=%async_computation.3 | async-start | bytes 2621440 | tf_op jit(solution)/shard_map/all_gather | solution.py:90
  44.9 88.8 %all-reduce.2.cloned.1.call-start = ((), (), s32[]{:S(2)}) async-start(), calls=%async_computation.4 | async-start | bytes 1048576 | tf_op jit(solution)/shard_map/psum | solution.py:97
  70.6 1.4 slice-start
  76.9 18.8 %copy-start.4 = (bf16[64,512]{1,0:T(8,128)(2,1)S(1)}, bf16[64,512]{1,0:T(8,128)(2,1)}, u32[]{:S(2)}) copy-start(bf16[64,512]{1,0:T(8,128)(2,1)} %param.22) | copy-start | bytes 196612
  95.8 0.8 copy-start.2
  96.6 313.5 %all-gather.9.cloned.1.call-start = ((), (), s32[]{:S(2)}) async-start(), calls=%async_computation.5 | async-start | bytes 57671680 | tf_op jit(solution)/shard_map/all_gather | solution.py:101
  97.2 588.0 %all-gather.11.cloned.1.call-start = ((), (), s32[]{:S(2)}) async-start(), calls=%async_computation.6 | async-start | bytes 57671680 | tf_op jit(solution)/shard_map/all_gather | solution.py:102
  97.8 0.7 copy-start.5
  97.8 37.1 %copy-start.6 = (f32[2048]{0:T(1024)S(1)}, f32[2048]{0:T(1024)}, u32[]{:S(2)}) copy-start(f32[2048]{0:T(1024)} %param.24) | copy-start | bytes 24580
  97.8 862.5 %all-gather.13.cloned.1.call-start = ((), (), s32[]{:S(2)}) async-start(), calls=%async_computation.7 | async-start | bytes 57671680 | tf_op jit(solution)/shard_map/all_gather | solution.py:103
  1024.8 4.7 copy-start.7
  1024.8 52.4 %all-to-all-start.2 = ((bf16[4,2,131072]{2,1,0:T(2,128)(2,1)}), bf16[4,2,131072]{2,1,0:T(2,128)(2,1)S(1)}, u32[]{:S(2)}, u32[]{:S(2)}) async-start(bf16[4,2,131072]{2,1,0:T(2,128)(2,1)} %reshape.199), calls=%async_computation.2 | async-start | bytes 4194304 | tf_op jit(solution)/shard_map/all_to_all | solution.py:125
  1093.5 3.7 copy-start.1
Sparse Core Ops, SparseCore 0:
  44.3 25.1 all-gather.14
  71.0 22.6 all-gather.6
  96.8 36.9 all-reduce.1
  135.1 274.9 all-gather.8
  411.6 273.5 all-gather.10
  686.7 273.5 all-gather.12
where the time goes:
time: 1110 us; the launch traced here: 1100 us
  waiting for transfers between devices  844 us (76%)
  matrix products  84 us (8%)
  local copies, waits for them, and re-layouts  67.6 us (6%)
  blocking collectives  66.4 us (6%)
  other arithmetic  23.1 us (2%)
  between operations  14.2 us (1%)
    all_gather x1, waiting for transfers between devices, body(): lax.all_gather(w_up, 'ctx', axis=1, tiled=True)  250 us
    all_gather x1, waiting for transfers between devices, body(): lax.all_gather(w_down, 'ctx', axis=2, tiled=True)  250 us
    all_gather x1, waiting for transfers between devices, body(): lax.all_gather(w_gate, 'ctx', axis=1, tiled=True)  237 us
    all_to_all x1, waiting for transfers between devices, body(): lax.all_to_all(lax.all_to_all(expert_out, 'req', split_axis=0, concat_axi...  47.6 us
    psum x1, waiting for transfers between devices, body(): hidden = lax.psum(partial_value, 'tp')  33.2 us
    all_to_all x1, blocking collectives, body(): lax.all_to_all(outgoing, 'req', split_axis=0, concat_axis=0, tiled=True)  27.5 us
    all_to_all x1, blocking collectives, body(): lax.all_to_all(expert_out, 'req', split_axis=0, concat_axis=0, tiled=True)  27.3 us
    dot_general x1, matrix products, body(): jnp.einsum('resd,edf->resf', gathered, full_up, preferred_element_type=jn...  25 us
  transfers between devices with their start and end apart: 7, of which 7 were waited for; matrix products, arithmetic and copies ran while one was open for 7% of the time, Pallas kernels for 0%

commit v1 on v0

v1 whole, which is shorter than its diff:
```python
import jax
import jax.numpy as jnp
from jax import lax
from jax.sharding import PartitionSpec as P

TOP = 6
CAP = 8
MASKED = -1e30


def attention_part(queries, new_keys, new_values, cache_keys, cache_values, length):
    ctx_pos, ctx_count = lax.axis_index("ctx"), lax.axis_size("ctx")
    tok_dev, heads, hd = queries.shape
    cache_dev = cache_keys.shape[1]
    block = tok_dev // ctx_count
    rows = heads * block
    q = queries.reshape(ctx_count, block, heads, hd).transpose(0, 2, 1, 3)
    q = q.reshape(ctx_count * rows, hd)
    keys = jnp.concatenate([cache_keys[0, :, 0, :], new_keys[:, 0, :]], 0)
    values = jnp.concatenate([cache_values[0, :, 0, :], new_values[:, 0, :]], 0)
    scores = jnp.dot(keys, q.T, preferred_element_type=jnp.float32) * (hd**-0.5)
    key_at = jnp.arange(cache_dev + tok_dev, dtype=jnp.int32)[:, None]
    row_at = jnp.arange(ctx_count * rows, dtype=jnp.int32)[None, :]
    token = (row_at // rows) * block + row_at % block
    valid = jnp.where(
        key_at < cache_dev,
        ctx_pos * cache_dev + key_at < length,
        jnp.logical_and(ctx_pos == ctx_count - 1, key_at - cache_dev <= token),
    )
    scores = jnp.where(valid, scores, MASKED)
    top = jnp.max(scores, 0, keepdims=True)
    weights = jnp.where(valid, jnp.exp(scores - top), 0.0)
    total = jnp.sum(weights, 0, keepdims=True)
    sums = lax.dot_general(
        values,
        weights.astype(jnp.bfloat16),
        (((0,), (0,)), ((), ())),
        preferred_element_type=jnp.float32,
    )
    pack = jnp.concatenate([sums, top, total, jnp.zeros((6, ctx_count * rows), jnp.float32)], 0)
    return pack.reshape(hd + 8, ctx_count, rows).transpose(1, 0, 2)


def merge(packs, hd, heads):
    top = jnp.max(packs[:, hd : hd + 1], 0)
    factor = jnp.exp(packs[:, hd : hd + 1] - top)
    total = jnp.sum(factor * packs[:, hd + 1 : hd + 2], 0)
    out = (jnp.sum(factor * packs[:, :hd], 0) / total).astype(jnp.bfloat16)
    block = out.shape[1] // heads
    return out.reshape(hd, heads, block).transpose(2, 1, 0).reshape(block, heads * hd)


def route_tables(expert_ids, gate_weights, exp_dev):
    block = expert_ids.shape[0]
    both = jnp.concatenate([expert_ids.astype(jnp.float32), gate_weights], 1)
    both = lax.all_gather(both, ("req", "ctx"))
    blocks = both.shape[0]
    ids = both[:, :, :TOP].astype(jnp.int32)
    gates = both[:, :, TOP:]
    first = lax.axis_index("req") * exp_dev
    experts = first + jnp.arange(exp_dev, dtype=jnp.int32)
    hits = ids[:, :, :, None] == experts
    gate_at = jnp.sum(jnp.where(hits, gates[..., None], 0.0), 2)
    hit = jnp.any(hits, 2)
    earlier = jnp.tril(jnp.ones((block, block), jnp.bfloat16), -1)
    rank = jnp.einsum(
        "ij,bje->bie", earlier, hit.astype(jnp.bfloat16), preferred_element_type=jnp.float32
    )
    code = jnp.arange(blocks, dtype=jnp.int32)[:, None, None] * CAP + rank.astype(jnp.int32)
    code = jnp.where(hit, code, -1)
    flat = (blocks * block, exp_dev)
    return code.reshape(flat).T, gate_at.reshape(flat).T


def body(
    queries,
    new_keys,
    new_values,
    cache_keys,
    cache_values,
    cache_lengths,
    residual,
    out_weight,
    norm_gain,
    expert_ids,
    gate_weights,
    w_gate,
    w_up,
    w_down,
):
    ctx_pos, tp_pos, req_pos = (lax.axis_index(a) for a in ("ctx", "tp", "req"))
    ctx_count, req_count = lax.axis_size("ctx"), lax.axis_size("req")
    tok_dev, heads, hd = queries.shape
    block, share = residual.shape
    exp_dev = w_gate.shape[0]
    slots = req_count * ctx_count * CAP
    length = lax.dynamic_index_in_dim(cache_lengths, req_pos, 0, keepdims=False)
    code, gate_at = route_tables(expert_ids, gate_weights, exp_dev)
    swap = [(a * ctx_count + b, b * ctx_count + a) for a in range(ctx_count) for b in range(ctx_count)]
    residual_t = lax.ppermute(residual, ("ctx", "tp"), swap)
    packs = attention_part(queries, new_keys, new_values, cache_keys, cache_values, length)
    packs = lax.all_to_all(packs, "ctx", 0, 0, tiled=True)
    attended = merge(packs, hd, heads)
    attended = lax.all_gather(attended, "ctx", tiled=True)
    part = jnp.dot(attended, out_weight, preferred_element_type=jnp.float32)
    part = part.reshape(-1, block, share)
    part = lax.all_to_all(part, "tp", 0, 0, tiled=True)
    hidden = jnp.sum(part, 0) + residual_t.astype(jnp.float32)
    squares = jnp.sum(hidden * hidden, 1)
    gain = lax.dynamic_slice_in_dim(norm_gain, ctx_pos * share, share, 0)
    scaled = (hidden * gain).astype(jnp.bfloat16)
    squares = lax.psum(squares, "ctx")
    factor = lax.rsqrt(squares / norm_gain.shape[0] + 1e-6)
    factor = lax.all_gather(factor, ("req", "tp"), tiled=True)
    scaled = lax.all_gather(scaled, ("req", "tp"), tiled=True)
    pick = code[:, None, :] == jnp.arange(slots, dtype=jnp.int32)[None, :, None]
    row_factor = jnp.sum(jnp.where(pick, factor, 0.0), -1, keepdims=True)
    row_gate = jnp.sum(jnp.where(pick, gate_at[:, None, :], 0.0), -1, keepdims=True)
    pick = pick.astype(jnp.bfloat16)
    rows = jnp.einsum("est,td->esd", pick, scaled, preferred_element_type=jnp.bfloat16)
    gate = jnp.einsum("esd,edf->esf", rows, w_gate, preferred_element_type=jnp.float32)
    up = jnp.einsum("esd,edf->esf", rows, w_up, preferred_element_type=jnp.float32)
    both = jnp.stack([gate, up], 2).astype(jnp.bfloat16)
    both = both.reshape(ctx_count, exp_dev * slots // ctx_count, 2, -1)
    both = lax.all_to_all(both, "ctx", 0, 0, tiled=True)
    both = both.astype(jnp.float32).sum(0)
    per = exp_dev * slots // ctx_count
    mine = lax.dynamic_slice_in_dim(row_factor.reshape(-1, 1), ctx_pos * per, per, 0)
    inner = (jax.nn.silu(both[:, 0] * mine) * (both[:, 1] * mine)).astype(jnp.bfloat16)
    inner = lax.all_gather(inner, "ctx", tiled=True).reshape(exp_dev, slots, -1)
    down = jnp.einsum("esf,efd->esd", inner, w_down, preferred_element_type=jnp.float32)
    down = (down * row_gate).astype(jnp.bfloat16)
    mixed = jnp.einsum("est,esd->td", pick, down, preferred_element_type=jnp.float32)
    mixed = mixed.astype(jnp.bfloat16).reshape(-1, block, share)
    mixed = lax.all_to_all(mixed, ("req", "tp"), 0, 0, tiled=True)
    out = hidden + jnp.sum(mixed.astype(jnp.float32), 0)
    return lax.ppermute(out.astype(jnp.bfloat16), ("ctx", "tp"), swap)


def solution(mesh):
    in_specs = (
        P("req", "tp", None),
        P("req", "tp", None),
        P("req", "tp", None),
        P("req", "ctx", "tp", None),
        P("req", "ctx", "tp", None),
        P(),
        P(("req", "ctx"), "tp"),
        P("tp", "ctx"),
        P(),
        P(("req", "ctx"), None),
        P(("req", "ctx"), None),
        P("req", "ctx", "tp"),
        P("req", "ctx", "tp"),
        P("req", "tp", "ctx"),
    )
    out_specs = P(("req", "ctx"), "tp")
    return jax.shard_map(body, mesh=mesh, in_specs=in_specs, out_specs=out_specs, check_vma=False)
```

time: 1110 us -> 256 us (0.23)
  waiting for transfers between devices: 844 us -> 36.9 us
  local copies, waits for them, and re-layouts: 67.6 us -> 10.6 us
  matrix products: 84 us -> 38.6 us
  blocking collectives: 66.4 us -> 111 us
  starting transfers between devices: 4.9 us -> 27.1 us
    all_gather x5 -> x1, waiting for transfers between devices: 761 us -> 22.8 us  [body(): inner = lax.all_gather(inner, 'ctx', tiled=True).reshape(exp_dev, slots, -1)]
    dot_general x6 -> x8, matrix products: 84 us -> 38.6 us  [the longest x1 8.61 us: body(): jnp.einsum('esd,edf->esf', rows, w_up, preferred_element_type=jnp.float32)]
    all_to_all x1 -> x3, waiting for transfers between devices: 47.6 us -> 11.6 us  [the longest x1 11.6 us: body(): part = lax.all_to_all(part, 'tp', 0, 0, tiled=True)]
    all_to_all x2 -> x1, blocking collectives: 54.8 us -> 19.7 us  [body(): mixed = lax.all_to_all(mixed, ('req', 'tp'), 0, 0, tiled=True)]
    psum x1 -> x0, waiting for transfers between devices: 33.2 us -> none  [body(): hidden = lax.psum(partial_value, 'tp')]
    psum x0 -> x1, blocking collectives: none -> 32.9 us  [body(): squares = lax.psum(squares, 'ctx')]
    all_gather x2 -> x3, blocking collectives: 11.6 us -> 43.8 us  [the longest x1 26.9 us: body(): scaled = lax.all_gather(scaled, ('req', 'tp'), tiled=True)]
    all_to_all x1 -> x3, starting transfers between devices: 4.7 us -> 20.3 us  [the longest x1 10.7 us: body(): both = lax.all_to_all(both, 'ctx', 0, 0, tiled=True)]
  transfers between devices with their start and end apart: 7 -> 6, of which waited for: 7 -> 3; matrix products, arithmetic and copies ran while one was open for 7% -> 2% of each run, Pallas kernels for 0% -> 0%
where the time goes in v1:
time: 256 us; the launch traced here: 253 us
  blocking collectives  111 us (43%)
  matrix products  38.6 us (15%)
  waiting for transfers between devices  36.9 us (14%)
  starting transfers between devices  27.1 us (11%)
  between operations  14.4 us (6%)
  other arithmetic  14 us (5%)
  local copies, waits for them, and re-layouts  10.6 us (4%)
    psum x1, blocking collectives, body(): squares = lax.psum(squares, 'ctx')  32.9 us
    all_gather x1, blocking collectives, body(): scaled = lax.all_gather(scaled, ('req', 'tp'), tiled=True)  26.9 us
    all_gather x1, waiting for transfers between devices, body(): inner = lax.all_gather(inner, 'ctx', tiled=True).reshape(exp_dev, slots, -1)  22.8 us
    all_to_all x1, blocking collectives, body(): mixed = lax.all_to_all(mixed, ('req', 'tp'), 0, 0, tiled=True)  19.7 us
    unnamed x1, blocking collectives  15.1 us
    all_to_all x1, waiting for transfers between devices, body(): part = lax.all_to_all(part, 'tp', 0, 0, tiled=True)  11.6 us
    all_gather x1, blocking collectives, route_tables(): both = lax.all_gather(both, ('req', 'ctx'))  11 us
    all_to_all x1, starting transfers between devices, body(): both = lax.all_to_all(both, 'ctx', 0, 0, tiled=True)  10.7 us
  transfers between devices with their start and end apart: 6, of which 3 were waited for; matrix products, arithmetic and copies ran while one was open for 2% of the time, Pallas kernels for 0%

profile of v1, /device:TPU:1, one launch (start us, length us, event | category | flops | bytes accessed | tf_op | source)
XLA Modules:
  0.0 253.1 jit_solution(7631431469196999747)
XLA Ops:
  9.5 6.5 %fusion = (f32[1024]{0:T(1024)S(1)}, f32[2304,1024]{1,0:T(8,128)S(1)}) fusion(s32[1024]{0:T(1024)S(1)} %fusion.38, s32[2304]{0:T(1024)S(1)} %iota_add_fusion, pred[2304]{0:T(1024)(128)(4,1)S(1)} %get-tuple-element.17, pred[2304]{0:T(1024)(128)(4,1)S(1)} %get-tuple-element.18, pred[]{:T(512)S(6)} %eq.16, bf16[1024,128]{1,0:T(8,128)(2,1)S(1)} %bitcast.83, ...), kind=kOutput, calls=%fused_computation.3 | convolution fusion | flops 619314176 | bytes 10311169 | tf_op jit(solution)/shard_map/dot_general | solution.py:21
  16.0 4.7 %fusion.1 = f32[1024]{0:T(1024)S(1)} fusion(f32[2304,1024]{1,0:T(8,128)S(1)} %get-tuple-element.16, f32[1024]{0:T(1024)S(1)} %get-tuple-element.15, s32[1024]{0:T(1024)S(1)} %fusion.38, s32[2304]{0:T(1024)S(1)} %iota_add_fusion, pred[2304]{0:T(1024)(128)(4,1)S(1)} %get-tuple-element.17, pred[2304]{0:T(1024)(128)(4,1)S(1)} %get-tuple-element.18, pred[]{:T(512)S(6)} %eq.16), kind=kLoop, calls=%fused_computation.5 | loop fusion | flops 18873344 | bytes 9463297 | tf_op jit(solution)/shard_map/reduce_sum | solution.py:33
  20.8 4.0 %fusion.3 = f32[128,1024]{1,0:T(8,128)S(1)} fusion(f32[2304,1024]{1,0:T(8,128)S(1)} %get-tuple-element.16, f32[1024]{0:T(1024)S(1)} %get-tuple-element.15, s32[1024]{0:T(1024)S(1)} %fusion.38, s32[2304]{0:T(1024)S(1)} %iota_add_fusion, pred[2304]{0:T(1024)(128)(4,1)S(1)} %get-tuple-element.17, pred[2304]{0:T(1024)(128)(4,1)S(1)} %get-tuple-element.18, ...), kind=kOutput, calls=%fused_computation.7 | convolution fusion | flops 624033792 | bytes 10573313 | tf_op jit(solution)/shard_map/dot_general | solution.py:34
  25.9 4.3 %all-to-all-start = ((f32[4,136,256]{2,1,0:T(8,128)}), f32[4,136,256]{2,1,0:T(8,128)S(1)}, u32[]{:S(2)}, u32[]{:S(2)}) async-start(f32[4,136,256]{2,1,0:T(8,128)} %maximum_bitcast_fusion), calls=%async_computation | async-start | bytes 1114112 | tf_op jit(solution)/shard_map/all_to_all | solution.py:102
  30.2 3.8 %collective-permute-start = (bf16[64,512]{1,0:T(8,128)(2,1)S(1)}, bf16[64,512]{1,0:T(8,128)(2,1)S(1)}, u32[]{:S(2)}, u32[]{:S(2)}) collective-permute-start(bf16[64,512]{1,0:T(8,128)(2,1)S(1)} %copy-done.14), channel_id=1, source_target_pairs={{0,0},{1,4},{2,8},{3,12},{4,1},{5,5},{6,9},{7,13},{8,2},{9,6},{10,... | collective-permute-start | bytes 196616 | tf_op jit(solution)/shard_map/ppermute | solution.py:100
  34.0 11.0 %all-gather.1 = f32[8,64,12]{1,2,0:T(8,128)S(1)} all-gather(f32[1,64,12]{1,2,0:T(8,128)S(1)} %maximum_bitcast_fusion.1), channel_id=2, replica_groups=mesh['req'=2,'ctx'=4,'tp'=4] {'req','ctx'}, dimensions={0}, use_global_device_ids=true | all-gather | bytes 27648 | tf_op jit(solution)/shard_map/all_gather | solution.py:56
  45.4 5.9 %all_gather.18 = bf16[256,512]{1,0:T(8,128)(2,1)S(1)} all-gather(bf16[64,512]{1,0:T(8,128)(2,1)S(1)} %copy_bitcast_fusion.1), channel_id=1, replica_groups=mesh['req'=2,'ctx'=4,'tp'=4] {'ctx'}, dimensions={0}, use_global_device_ids=true | all-gather | bytes 327680 | tf_op jit(solution)/shard_map/all_gather | solution.py:104
  52.4 5.3 %all-to-all-start.1 = ((f32[4,64,512]{2,1,0:T(8,128)}), f32[4,64,512]{2,1,0:T(8,128)S(1)}, u32[]{:S(2)}, u32[]{:S(2)}) async-start(f32[4,64,512]{2,1,0:T(8,128)} %bitcast.13), calls=%async_computation.1 | async-start | bytes 1048576 | tf_op jit(solution)/shard_map/all_to_all | solution.py:107
  60.3 11.6 %all-to-all-done.1 = f32[4,64,512]{2,1,0:T(8,128)S(1)} async-done(((f32[4,64,512]{2,1,0:T(8,128)}), f32[4,64,512]{2,1,0:T(8,128)S(1)}, u32[]{:S(2)}, u32[]{:S(2)}) %all-to-all-start.1) | async-done | bytes 524320 | tf_op jit(solution)/shard_map/all_to_all | solution.py:107
  72.0 26.9 %all_gather.21 = bf16[512,512]{1,0:T(8,128)(2,1)S(1)} all-gather(bf16[64,512]{1,0:T(8,128)(2,1)S(1)} %get-tuple-element.12), channel_id=1, replica_groups=mesh['req'=2,'ctx'=4,'tp'=4] {'req','tp'}, dimensions={0}, use_global_device_ids=true | all-gather | bytes 589824 | tf_op jit(solution)/shard_map/all_gather | solution.py:115
  100.2 8.6 %convolution_convert_fusion = bf16[32,64,352]{2,1,0:T(8,128)(2,1)} fusion(bf16[32,64,512]{2,1,0:T(8,128)(2,1)S(1)} %fusion.6, bf16[32,512,352]{1,2,0:T(8,128)(2,1)} %param.26), kind=kOutput, calls=%fused_computation.17 | convolution fusion | flops 738918400 | bytes 15073280 | tf_op jit(solution)/shard_map/esd,edf->esf/dot_general | solution.py:122
  108.8 2.5 %copy.63 = bf16[4,512,1,352]{1,3,2,0:T(8,128)(2,1)} copy(bf16[4,512,1,352]{3,1,0,2:T(8,128)(2,1)} %bitcast.77) | data formatting | bytes 2883584 | tf_op jit(solution)/shard_map/stack | solution.py:123
  111.4 8.6 %convolution_convert_fusion.1 = bf16[32,64,352]{2,1,0:T(8,128)(2,1)} fusion(bf16[32,64,512]{2,1,0:T(8,128)(2,1)S(1)} %fusion.6, bf16[32,512,352]{1,2,0:T(8,128)(2,1)} %param.25), kind=kOutput, calls=%fused_computation.18 | convolution fusion | flops 738918400 | bytes 15073280 | tf_op jit(solution)/shard_map/esd,edf->esf/dot_general | solution.py:121
  120.0 1.7 copy.62
  121.7 3.2 %pad_maximum_fusion = bf16[4,512,2,352]{1,3,2,0:T(8,128)(2,1)} fusion(bf16[4,512,1,352]{1,3,2,0:T(8,128)(2,1)} %copy.63, bf16[4,512,1,352]{1,3,2,0:T(8,128)(2,1)S(1)} %copy.62), kind=kLoop, calls=%fused_computation.14 | loop fusion | flops 1441792 | bytes 5767168 | tf_op jit(solution)/shard_map/stack | solution.py:123
  124.9 10.7 %all-to-all-start.2 = ((bf16[4,512,2,352]{1,3,2,0:T(8,128)(2,1)}), bf16[4,512,2,352]{1,3,2,0:T(8,128)(2,1)S(1)}, u32[]{:S(2)}, u32[]{:S(2)}) async-start(bf16[4,512,2,352]{1,3,2,0:T(8,128)(2,1)} %pad_maximum_fusion), calls=%async_computation.2 | async-start | bytes 5767168 | tf_op jit(solution)/shard_map/all_to_all | solution.py:125
  137.3 32.9 %psum.7 = f32[64]{0:T(128)S(1)} all-reduce(f32[64]{0:T(128)S(1)} %get-tuple-element.11), channel_id=1, replica_groups=mesh['req'=2,'ctx'=4,'tp'=4] {'ctx'}, use_global_device_ids=true, to_apply=%region_9.10 | all-reduce | flops 64 | bytes 512 | tf_op jit(solution)/shard_map/psum | solution.py:112
  170.3 15.1 %all-reduce = f32[512]{0:T(512)S(1)} all-reduce(f32[512]{0:T(512)S(1)} %rsqrt_dynamic-update-slice_fusion), channel_id=1, replica_groups=mesh['req'=2,'ctx'=4,'tp'=4] {'req','tp'}, use_global_device_ids=true, to_apply=%add | all-reduce | flops 512 | bytes 4096
  185.4 1.5 select_reduce_fusion
  189.1 22.8 %all-gather.4.cloned.1.call-done = bf16[2048,352]{1,0:T(8,128)(2,1)} async-done(((bf16[512,352]{1,0:T(8,128)(2,1)}), bf16[2048,352]{1,0:T(8,128)(2,1)}) %all-gather.4.cloned.1.call-update) | async-done | bytes 1441808 | tf_op jit(solution)/shard_map/all_gather | solution.py:130
  212.0 8.3 %fusion.10 = bf16[512,512]{1,0:T(8,128)(2,1)S(1)} fusion(s32[32,512]{1,0:T(8,128)S(1)} %bitcast.86, bf16[32,64,352]{2,1,0:T(8,128)(2,1)} %bitcast.92, bf16[32,352,512]{2,1,0:T(8,128)(2,1)} %param.27, f32[32,64]{1,0:T(8,128)S(1)} %get-tuple-element.5), kind=kOutput, calls=%fused_computation.20 | convolution fusion | flops 1815347200 | bytes 13574144 | tf_op jit(solution)/shard_map/est,esd->td/dot_general | solution.py:133
  220.2 19.7 %all_to_all.20 = bf16[8,64,512]{2,1,0:T(8,128)(2,1)S(1)} all-to-all(bf16[8,64,512]{2,1,0:T(8,128)(2,1)S(1)} %bitcast.81), channel_id=1, replica_groups=mesh['req'=2,'ctx'=4,'tp'=4] {'req','tp'}, dimensions={0} | all-to-all | bytes 1048576 | tf_op jit(solution)/shard_map/all_to_all | solution.py:135
  240.0 3.1 %collective-permute-start.1 = (bf16[64,512]{1,0:T(8,128)(2,1)S(1)}, bf16[64,512]{1,0:T(8,128)(2,1)S(1)}, u32[]{:S(2)}, u32[]{:S(2)}) collective-permute-start(bf16[64,512]{1,0:T(8,128)(2,1)S(1)} %add_convert_fusion), channel_id=1, source_target_pairs={{0,0},{1,4},{2,8},{3,12},{4,1},{5,5},{6,9},{7,13},{8,2},{9,6},{10,... | collective-permute-start | bytes 196616 | tf_op jit(solution)/shard_map/ppermute | solution.py:137
  243.1 2.5 collective-permute-done.1
  (85 shorter events, 13.6 us)
Async XLA Ops:
  6.5 44.8 %copy-start = (bf16[512,512]{1,0:T(8,128)(2,1)S(1)}, bf16[512,512]{1,0:T(8,128)(2,1)}, u32[]{:S(2)}) copy-start(bf16[512,512]{1,0:T(8,128)(2,1)} %param.21) | copy-start | bytes 1572868
  16.0 4.8 %copy-start.12 = (bf16[1,2048,1,128]{3,1,2,0:T(8,128)(2,1)S(1)}, bf16[1,2048,1,128]{3,1,2,0:T(8,128)(2,1)}, u32[]{:S(2)}) copy-start(bf16[1,2048,1,128]{3,1,2,0:T(8,128)(2,1)} %param.18) | copy-start | bytes 1572868
  16.0 4.8 %copy-start.13 = (bf16[256,1,128]{2,0,1:T(8,128)(2,1)S(1)}, bf16[256,1,128]{2,0,1:T(8,128)(2,1)}, u32[]{:S(2)}) copy-start(bf16[256,1,128]{2,0,1:T(8,128)(2,1)} %param.16) | copy-start | bytes 196612
  20.8 9.4 %copy-start.14 = (bf16[64,512]{1,0:T(8,128)(2,1)S(1)}, bf16[64,512]{1,0:T(8,128)(2,1)}, u32[]{:S(2)}) copy-start(bf16[64,512]{1,0:T(8,128)(2,1)} %param.20) | copy-start | bytes 196612
  20.8 13.2 %copy-start.10 = (s32[64,6]{0,1:T(8,128)S(1)}, s32[64,6]{0,1:T(8,128)}, u32[]{:S(2)}) copy-start(s32[64,6]{0,1:T(8,128)} %param.23) | copy-start | bytes 4612
  20.8 13.2 %copy-start.11 = (f32[64,6]{0,1:T(8,128)S(1)}, f32[64,6]{0,1:T(8,128)}, u32[]{:S(2)}) copy-start(f32[64,6]{0,1:T(8,128)} %param.24) | copy-start | bytes 4612
  25.9 19.1 %all-to-all-start = ((f32[4,136,256]{2,1,0:T(8,128)}), f32[4,136,256]{2,1,0:T(8,128)S(1)}, u32[]{:S(2)}, u32[]{:S(2)}) async-start(f32[4,136,256]{2,1,0:T(8,128)} %maximum_bitcast_fusion), calls=%async_computation | async-start | bytes 1114112 | tf_op jit(solution)/shard_map/all_to_all | solution.py:102
  30.2 41.7 %collective-permute-start = (bf16[64,512]{1,0:T(8,128)(2,1)S(1)}, bf16[64,512]{1,0:T(8,128)(2,1)S(1)}, u32[]{:S(2)}, u32[]{:S(2)}) collective-permute-start(bf16[64,512]{1,0:T(8,128)(2,1)S(1)} %copy-done.14), channel_id=1, source_target_pairs={{0,0},{1,4},{2,8},{3,12},{4,1},{5,5},{6,9},{7,13},{8,2},{9,6},{10,... | collective-permute-start | bytes 196616 | tf_op jit(solution)/shard_map/ppermute | solution.py:100
  52.4 19.5 %all-to-all-start.1 = ((f32[4,64,512]{2,1,0:T(8,128)}), f32[4,64,512]{2,1,0:T(8,128)S(1)}, u32[]{:S(2)}, u32[]{:S(2)}) async-start(f32[4,64,512]{2,1,0:T(8,128)} %bitcast.13), calls=%async_computation.1 | async-start | bytes 1048576 | tf_op jit(solution)/shard_map/all_to_all | solution.py:107
  58.3 0.6 copy-start.2
  59.5 49.3 %copy-start.4 = (s32[512,32]{0,1:T(8,128)}, s32[512,32]{0,1:T(8,128)S(1)}, u32[]{:S(2)}) copy-start(s32[512,32]{0,1:T(8,128)S(1)} %reshape.144) | copy-start | bytes 196612
  71.9 36.9 %copy-start.7 = (bf16[64,512]{1,0:T(8,128)(2,1)}, bf16[64,512]{1,0:T(8,128)(2,1)S(1)}, u32[]{:S(2)}) copy-start(bf16[64,512]{1,0:T(8,128)(2,1)S(1)} %collective-permute-done) | copy-start | bytes 196612
  124.9 10.7 %copy-start.3 = (s32[8,64,6]{1,2,0:T(8,128)S(1)}, s32[8,64,6]{1,2,0:T(8,128)}, u32[]{:S(2)}) copy-start(s32[8,64,6]{1,2,0:T(8,128)} %copy-done.2) | copy-start | bytes 36868
  124.9 10.7 %copy-start.9 = (f32[8,64,6]{1,2,0:T(8,128)S(1)}, f32[8,64,6]{1,2,0:T(8,128)}, u32[]{:S(2)}) copy-start(f32[8,64,6]{1,2,0:T(8,128)} %get-tuple-element.13) | copy-start | bytes 36868
  124.9 11.1 %copy-start.15 = (u32[32]{0:T(128)S(1)}, u32[32]{0:T(128)}, u32[]{:S(2)}) copy-start(u32[32]{0:T(128)} %constant.96) | copy-start | bytes 388
  124.9 60.4 %copy-start.5 = (s32[512,32]{0,1:T(8,128)S(1)}, s32[512,32]{0,1:T(8,128)}, u32[]{:S(2)}) copy-start(s32[512,32]{0,1:T(8,128)} %copy-done.4) | copy-start | bytes 196612
  124.9 62.0 %all-to-all-start.2 = ((bf16[4,512,2,352]{1,3,2,0:T(8,128)(2,1)}), bf16[4,512,2,352]{1,3,2,0:T(8,128)(2,1)S(1)}, u32[]{:S(2)}, u32[]{:S(2)}) async-start(bf16[4,512,2,352]{1,3,2,0:T(8,128)(2,1)} %pad_maximum_fusion), calls=%async_computation.2 | async-start | bytes 5767168 | tf_op jit(solution)/shard_map/all_to_all | solution.py:125
  135.6 76.3 %all-gather.4.cloned.1.call-start = ((), (), s32[]{:S(2)}) async-start(), calls=%async_computation.4 | async-start | bytes 1966080 | tf_op jit(solution)/shard_map/all_gather | solution.py:130
  187.4 24.5 %copy-start.6 = (s32[512,32]{0,1:T(8,128)S(1)}, s32[512,32]{0,1:T(8,128)}, u32[]{:S(2)}) copy-start(s32[512,32]{0,1:T(8,128)} %copy-done.4) | copy-start | bytes 196612
  212.0 28.0 %copy-start.8 = (bf16[64,512]{1,0:T(8,128)(2,1)S(1)}, bf16[64,512]{1,0:T(8,128)(2,1)}, u32[]{:S(2)}) copy-start(bf16[64,512]{1,0:T(8,128)(2,1)} %copy-done.7) | copy-start | bytes 196612
  212.0 34.3 %copy-start.1 = (bf16[512,512]{1,0:T(8,128)(2,1)S(1)}, bf16[512,512]{1,0:T(8,128)(2,1)}, u32[]{:S(2)}) copy-start(bf16[512,512]{1,0:T(8,128)(2,1)} %param.21) | copy-start | bytes 1572868
  240.0 5.6 %collective-permute-start.1 = (bf16[64,512]{1,0:T(8,128)(2,1)S(1)}, bf16[64,512]{1,0:T(8,128)(2,1)S(1)}, u32[]{:S(2)}, u32[]{:S(2)}) collective-permute-start(bf16[64,512]{1,0:T(8,128)(2,1)S(1)} %add_convert_fusion), channel_id=1, source_target_pairs={{0,0},{1,4},{2,8},{3,12},{4,1},{5,5},{6,9},{7,13},{8,2},{9,6},{10,... | collective-permute-start | bytes 196616 | tf_op jit(solution)/shard_map/ppermute | solution.py:137
Sparse Core Ops, SparseCore 0:
  189.3 22.6 all-gather.3

commit v2 on v1

--- a/solution.py
+++ b/solution.py
@@ -1,11 +1,566 @@
+import functools
 import jax
 import jax.numpy as jnp
 from jax import lax
+from jax.experimental import pallas as pl
+from jax.experimental.pallas import tpu as pltpu
 from jax.sharding import PartitionSpec as P
 
 TOP = 6
 CAP = 8
 MASKED = -1e30
+F32 = jnp.float32
+BF16 = jnp.bfloat16
+CHUNKS = 4
+FUSED_BYTES = 4 * 1024 * 1024
+
+
+def dot(a, b, contract, kind=F32):
+    return lax.dot_general(a, b, (contract, ((), ())), preferred_element_type=kind)
+
+
+def layer_kernel(
+    dims,
+    len_ref,
+    q_ref,
+    ck_ref,
+    cv_ref,
+    nk_ref,
+    nv_ref,
+    res_ref,
+    ow_ref,
+    gain_ref,
+    rt_ref,
+    wg_hbm,
+    wu_hbm,
+    wd_hbm,
+    out_ref,
+    wg,
+    wu,
+    wd,
+    pk_send,
+    pk_recv,
+    att,
+    part,
+    part_recv,
+    res_t,
+    hidden,
+    sq,
+    fac,
+    tab,
+    codes,
+    tok,
+    pick,
+    x,
+    gu,
+    r1,
+    s2,
+    r2,
+    inner,
+    ys,
+    acc,
+    mix,
+    mix_recv,
+    tsend,
+    trecv,
+    fin,
+    fin_recv,
+    w_sem,
+    ssem,
+    rsem,
+):
+    reqs, ctxs, tps, block, heads, hd, exp_dev, slots, ff, share = dims
+    r, c, t = lax.axis_index("req"), lax.axis_index("ctx"), lax.axis_index("tp")
+    blocks = reqs * ctxs
+    tokens = blocks * block
+    chunk = exp_dev * slots // CHUNKS
+    quarter = chunk // ctxs
+    rb = min(slots, quarter)
+    y, k = c // 2, c % 2
+    count = [0]
+
+    def rcopy(src, dst, **where):
+        i = count[0]
+        count[0] = i + 1
+        return pltpu.make_async_remote_copy(
+            src_ref=src,
+            dst_ref=dst,
+            send_sem=ssem.at[i],
+            recv_sem=rsem.at[i],
+            device_id={"req": r, "ctx": c, "tp": t} | where,
+            device_id_type=pl.DeviceIdType.MESH,
+        )
+
+    def step(me, d, n):
+        return lax.rem(me + d, n)
+
+    loads = [
+        pltpu.make_async_copy(wg_hbm, wg, w_sem.at[0]),
+        pltpu.make_async_copy(wu_hbm, wu, w_sem.at[1]),
+        pltpu.make_async_copy(wd_hbm, wd, w_sem.at[2]),
+    ]
+    for load in loads:
+        load.start()
+
+    barrier = pltpu.get_barrier_semaphore()
+    peers = [
+        {"req": step(r, a, reqs), "ctx": step(c, b, ctxs), "tp": t}
+        for a in range(reqs)
+        for b in range(ctxs)
+        if a or b
+    ] + [{"req": r, "ctx": c, "tp": step(t, d, tps)} for d in range(1, tps)]
+    swap = {"ctx": t, "tp": c}
+    for peer in peers:
+        pl.semaphore_signal(barrier, 1, device_id=peer, device_id_type=pl.DeviceIdType.MESH)
+
+    @pl.when(c != t)
+    def _():
+        pl.semaphore_signal(
+            barrier, 1, device_id={"req": r} | swap, device_id_type=pl.DeviceIdType.MESH
+        )
+        pl.semaphore_wait(barrier, len(peers) + 1)
+
+    @pl.when(c == t)
+    def _():
+        pl.semaphore_wait(barrier, len(peers))
+
+    pending = []
+
+    me = r * ctxs + c
+    tab_copies = []
+    for a in range(reqs):
+        for b in range(ctxs):
+            if a or b:
+                to = step(r, a, reqs)
+                copy = rcopy(rt_ref.at[to], tab.at[me], req=to, ctx=step(c, b, ctxs))
+                copy.start()
+                tab_copies.append(copy)
+    tab[me] = rt_ref[r]
+    res_copy = rcopy(res_ref, res_t, **swap)
+
+    @pl.when(c != t)
+    def _():
+        res_copy.start()
+
+    @pl.when(c == t)
+    def _():
+        res_t[...] = res_ref[...]
+
+    length = len_ref[r]
+    cache_dev, new_dev = ck_ref.shape[0], nk_ref.shape[0]
+    rows = heads * block
+    scale = hd**-0.5
+    old_at = lax.broadcasted_iota(jnp.int32, (cache_dev, rows), 0)
+    old_ok = old_at < length - c * cache_dev
+    new_at = lax.broadcasted_iota(jnp.int32, (new_dev, rows), 0)
+    lane = lax.broadcasted_iota(jnp.int32, (new_dev, rows), 1) % block
+    stat_at = lax.broadcasted_iota(jnp.int32, (8, rows), 0)
+    last = jnp.where(c == ctxs - 1, 0, new_dev)
+    pk_copies = []
+    for d in list(range(1, ctxs)) + [0]:
+        b = step(c, d, ctxs)
+        q = q_ref[b]
+        new_ok = new_at + last <= lane + b * block
+        old = jnp.where(old_ok, dot(ck_ref[...], q, ((1,), (1,))) * scale, MASKED)
+        new = jnp.where(new_ok, dot(nk_ref[...], q, ((1,), (1,))) * scale, MASKED)
+        top = jnp.maximum(
+            jnp.max(old, 0, keepdims=True), jnp.max(new, 0, keepdims=True)
+        )
+        old = jnp.where(old_ok, jnp.exp(old - top), 0.0)
+        new = jnp.where(new_ok, jnp.exp(new - top), 0.0)
+        total = jnp.sum(old, 0, keepdims=True) + jnp.sum(new, 0, keepdims=True)
+        sums = dot(cv_ref[...], old.astype(BF16), ((0,), (0,)))
+        sums = sums + dot(nv_ref[...], new.astype(BF16), ((0,), (0,)))
+        pk_send[d, 0:hd, :] = sums
+        pk_send[d, hd : hd + 8, :] = jnp.where(
+            stat_at == 0, top, jnp.where(stat_at == 1, total, 0.0)
+        )
+        if d:
+            copy = rcopy(pk_send.at[d], pk_recv.at[d], ctx=b)
+            copy.start()
+            pk_copies.append(copy)
+    for copy in pk_copies:
+        copy.wait_recv()
+    pending += pk_copies
+    packs = [pk_send.at[0]] + [pk_recv.at[d] for d in range(1, ctxs)]
+    tops = [p[hd : hd + 1, :] for p in packs]
+    top = functools.reduce(jnp.maximum, tops)
+    total = jnp.zeros((1, rows), F32)
+    sums = jnp.zeros((hd, rows), F32)
+    for p, own in zip(packs, tops):
+        factor = jnp.exp(own - top)
+        total = total + factor * p[hd + 1 : hd + 2, :]
+        sums = sums + factor * p[0:hd, :]
+    out = jnp.transpose(sums / total)
+    for h in range(heads):
+        att[c, :, h * hd : (h + 1) * hd] = out[h * block : (h + 1) * block].astype(BF16)
+    att_copies = []
+    for d in range(1, ctxs):
+        copy = rcopy(att.at[c], att.at[c], ctx=step(c, d, ctxs))
+        copy.start()
+        att_copies.append(copy)
+    for copy in tab_copies:
+        copy.wait_recv()
+    pending += tab_copies
+    for p in range(blocks // 2):
+        codes[:, p * 128 : (p + 1) * 128] = tab[2 * p] + tab[2 * p + 1]
+    slot_at = lax.broadcasted_iota(jnp.int32, (rb, tokens), 0).astype(F32)
+
+    def make_pick(i, carry):
+        row = i * rb
+        e = row // slots
+        code = codes[pl.ds(e, 1), :] - (row - e * slots + 1).astype(F32)
+        pick[pl.ds(pl.multiple_of(row, rb), rb), :] = jnp.where(
+            slot_at == code, 1.0, 0.0
+        ).astype(BF16)
+        return carry
+
+    lax.fori_loop(0, exp_dev * slots // rb, make_pick, 0)
+    for copy in att_copies:
+        copy.wait_recv()
+    pending += att_copies
+    width = heads * hd
+    full = dot(att[...].reshape(ctxs * block, width), ow_ref[...], ((1,), (0,)))
+    part[...] = full.reshape(tps, block, share)
+    part_copies = []
+    for d in range(1, tps):
+        to = step(t, d, tps)
+        copy = rcopy(part.at[to], part_recv.at[d], tp=to)
+        copy.start()
+        part_copies.append(copy)
+    hid = part[t]
+
+    @pl.when(c != t)
+    def _():
+        res_copy.wait_recv()
+
+    hid = hid + res_t[...].astype(F32)
+    for d in range(1, tps):
+        part_copies[d - 1].wait_recv()
+        hid = hid + part_recv[d]
+    pending += part_copies
+    hidden[...] = hid
+    tok[r * tps + t] = (hid * gain_ref[...]).astype(BF16)
+    tok_copies = []
+    for a in range(reqs):
+        for d in range(tps):
+            if (a == 0) and d:
+                copy = rcopy(tok.at[r * tps + t], tok.at[r * tps + t], tp=step(t, d, tps))
+                copy.start()
+                tok_copies.append(copy)
+    far_copies = []
+    for a in range(1, reqs):
+        copy = rcopy(tok.at[r * tps + t], tok.at[r * tps + t], req=step(r, a, reqs))
+        copy.start()
+        far_copies.append(copy)
+    sq[0] = jnp.broadcast_to(jnp.sum(hid * hid, 1, keepdims=True), (block, 128))
+    sq_copies = []
+    for d in range(1, ctxs):
+        copy = rcopy(sq.at[0], sq.at[d], ctx=step(c, d, ctxs))
+        copy.start()
+        sq_copies.append(copy)
+    for copy in sq_copies:
+        copy.wait_recv()
+    pending += sq_copies
+    squares = sq[0]
+    for d in range(1, ctxs):
+        squares = squares + sq[d]
+    fac[r * tps + t] = lax.rsqrt(squares / (share * ctxs) + 1e-6)
+    fac_copies = []
+    for d in range(1, tps):
+        copy = rcopy(fac.at[r * tps + t], fac.at[r * tps + t], tp=step(t, d, tps))
+        copy.start()
+        fac_copies.append(copy)
+    fac_far = []
+    for a in range(1, reqs):
+        copy = rcopy(fac.at[r * tps + t], fac.at[r * tps + t], req=step(r, a, reqs))
+        copy.start()
+        fac_far.append(copy)
+    for d in range(1, tps):
+        tok_copies[d - 1].wait_recv()
+        at = r * tps + step(t, tps - d, tps)
+        for a in range(1, reqs):
+            copy = rcopy(tok.at[at], tok.at[at], req=step(r, a, reqs))
+            copy.start()
+            far_copies.append(copy)
+    for d in range(1, tps):
+        fac_copies[d - 1].wait_recv()
+        at = r * tps + step(t, tps - d, tps)
+        for a in range(1, reqs):
+            copy = rcopy(fac.at[at], fac.at[at], req=step(r, a, reqs))
+            copy.start()
+            fac_far.append(copy)
+    for copy in far_copies:
+        copy.wait_recv()
+    pending += tok_copies + far_copies + fac_copies
+    loads[0].wait()
+    loads[1].wait()
+
+    n_sub = chunk // rb
+    n_q = quarter // rb
+    first, second, third, fourth = [], [], [], []
+
+    def up_stage(j):
+        base = j * chunk
+        x[...] = dot(
+            pick[base : base + chunk, :], tok[...].reshape(tokens, share), ((1,), (0,))
+        ).astype(BF16)
+
+        def one(i, carry):
+            e = (base + i * rb) // slots
+            at = pl.ds(pl.multiple_of((i % n_q) * rb, rb), rb)
+            xs = x[pl.ds(pl.multiple_of(i * rb, rb), rb), :]
+            q = i // n_q
+            gu[0, j, q // 2, q % 2, at, :] = dot(xs, wg[e], ((1,), (0,))).astype(BF16)
+            gu[1, j, q // 2, q % 2, at, :] = dot(xs, wu[e], ((1,), (0,))).astype(BF16)
+            return carry
+
+        lax.fori_loop(0, n_sub, one, 0)
+        copy = rcopy(gu.at[:, j, :, 1 - k], r1.at[:, j], ctx=y * 2 + 1 - k)
+        copy.start()
+        first.append(copy)
+
+    def pair_stage(j):
+        first[j].wait_recv()
+        s2[:, j] = (
+            gu[:, j, 1 - y, k].astype(F32) + r1[:, j, 1 - y].astype(F32)
+        ).astype(BF16)
+        copy = rcopy(s2.at[:, j], r2.at[:, j], ctx=(1 - y) * 2 + k)
+        copy.start()
+        second.append(copy)
+
+    def act_stage(j):
+        second[j].wait_recv()
+        both = gu[:, j, y, k].astype(F32) + r1[:, j, y].astype(F32) + r2[:, j].astype(F32)
+        col = lax.broadcasted_iota(jnp.int32, (tokens, 128), 1)
+        f = fac[...].reshape(tokens, 128)
+        hi = f.astype(BF16).astype(F32)
+        mid = (f - hi).astype(BF16).astype(F32)
+        low = f - hi - mid
+        f = jnp.where(col == 0, hi, jnp.where(col == 1, mid, jnp.where(col == 2, low, 0.0)))
+        mine = pick[pl.ds(pl.multiple_of(j * chunk + c * quarter, quarter), quarter), :]
+        row = jnp.sum(dot(mine, f.astype(BF16), ((1,), (0,))), 1, keepdims=True)
+        g = both[0] * row
+        inner[j, y, k] = (g * jax.nn.sigmoid(g) * (both[1] * row)).astype(BF16)
+        copy = rcopy(inner.at[j, y, k], inner.at[j, y, k], ctx=(1 - y) * 2 + k)
+        copy.start()
+        third.append(copy)
+
+    def share_stage(j):
+        third[j].wait_recv()
+        copy = rcopy(inner.at[j, :, k], inner.at[j, :, k], ctx=y * 2 + 1 - k)
+        copy.start()
+        fourth.append(copy)
+
+    def down_stage(j):
+        fourth[j].wait_recv()
+        base = j * chunk
+
+        def one(i, carry):
+            e = (base + i * rb) // slots
+            q = i // n_q
+            at = pl.ds(pl.multiple_of((i % n_q) * rb, rb), rb)
+            rows_at = pl.multiple_of(i * rb, rb)
+            down = dot(inner[j, q // 2, q % 2, at, :], wd[e], ((1,), (0,)))
+            mask = pick[pl.ds(pl.multiple_of(base + rows_at, rb), rb), :].astype(F32)
+            gate = jnp.sum(mask * codes[pl.ds(exp_dev + e, 1), :], 1, keepdims=True)
+            ys[pl.ds(rows_at, rb), :] = (down * gate).astype(BF16)
+            return carry
+
+        lax.fori_loop(0, n_sub, one, 0)
+        term = dot(pick[base : base + chunk, :], ys[...], ((0,), (0,)))
+        if j == 0:
+            acc[...] = term
+        else:
+            acc[...] += term
+
+    up_stage(0)
+    up_stage(1)
+    pair_stage(0)
+    up_stage(2)
+    for copy in fac_far:
+        copy.wait_recv()
+    pending.extend(fac_far)
+    act_stage(0)
+    pair_stage(1)
+    up_stage(3)
+    loads[2].wait()
+    share_stage(0)
+    act_stage(1)
+    pair_stage(2)
+    down_stage(0)
+    share_stage(1)
+    act_stage(2)
+    pair_stage(3)
+    down_stage(1)
+    share_stage(2)
+    act_stage(3)
+    down_stage(2)
+    share_stage(3)
+    down_stage(3)
+    pending += first + second + third + fourth
+
+    per = tps * block
+    mix_copies = []
+    for a in range(1, reqs):
+        to = step(r, a, reqs)
+        mix[a] = acc[pl.ds(pl.multiple_of(to * per, per), per), :].astype(BF16)
+        copy = rcopy(mix.at[a], mix_recv.at[a], req=to)
+        copy.start()
+        mix_copies.append(copy)
+    mixed = acc[pl.ds(pl.multiple_of(r * per, per), per), :]
+    for a in range(1, reqs):
+        mix_copies[a - 1].wait_recv()
+        mixed = mixed + mix_recv[a].astype(F32)
+    pending += mix_copies
+    tsend[...] = mixed.reshape(tps, block, share).astype(BF16)
+    t_copies = []
+    for d in range(1, tps):
+        to = step(t, d, tps)
+        copy = rcopy(tsend.at[to], trecv.at[d], tp=to)
+        copy.start()
+        t_copies.append(copy)
+    total = hidden[...] + tsend[t].astype(F32)
+    for d in range(1, tps):
+        t_copies[d - 1].wait_recv()
+        total = total + trecv[d].astype(F32)
+    pending += t_copies
+    fin[...] = total.astype(BF16)
+    fin_copy = rcopy(fin, fin_recv, **swap)
+
+    @pl.when(c != t)
+    def _():
+        fin_copy.start()
+        fin_copy.wait()
+        res_copy.wait_send()
+        out_ref[...] = fin_recv[...]
+
+    @pl.when(c == t)
+    def _():
+        out_ref[...] = fin[...]
+
+    for copy in pending:
+        copy.wait_send()
+
+
+def fused_body(
+    queries,
+    new_keys,
+    new_values,
+    cache_keys,
+    cache_values,
+    cache_lengths,
+    residual,
+    out_weight,
+    norm_gain,
+    expert_ids,
+    gate_weights,
+    w_gate,
+    w_up,
+    w_down,
+):
+    reqs, ctxs, tps = (lax.axis_size(a) for a in ("req", "ctx", "tp"))
+    r, c = lax.axis_index("req"), lax.axis_index("ctx")
+    tok_dev, heads, hd = queries.shape
+    block, share = residual.shape
+    exp_dev, _, ff = w_gate.shape
+    blocks = reqs * ctxs
+    slots = blocks * CAP
+    tokens = blocks * block
+    chunk = exp_dev * slots // CHUNKS
+    quarter = chunk // ctxs
+    rows = heads * block
+    q = queries.reshape(ctxs, block, heads, hd).transpose(0, 2, 1, 3).reshape(ctxs, rows, hd)
+    me = r * ctxs + c
+    experts = jnp.arange(reqs * exp_dev, dtype=jnp.int32)
+    hits = expert_ids[None, :, :] == experts[:, None, None]
+    gates = jnp.sum(jnp.where(hits, gate_weights[None], 0.0), 2)
+    hit = jnp.any(hits, 2)
+    later = jnp.triu(jnp.ones((block, block), BF16), 0)
+    rank = jnp.dot(hit.astype(BF16), later, preferred_element_type=F32)
+    code = jnp.where(hit, rank + (me * CAP).astype(F32), 0.0)
+    table = jnp.stack([code.reshape(reqs, exp_dev, block), gates.reshape(reqs, exp_dev, block)], 1)
+    table = table.reshape(reqs, 2 * exp_dev, block)
+    zero = jnp.zeros_like(table)
+    odd = me % 2 == 1
+    table = jnp.concatenate([jnp.where(odd, zero, table), jnp.where(odd, table, zero)], 2)
+    gain = lax.dynamic_slice_in_dim(norm_gain, c * share, share, 0).reshape(1, share)
+    dims = (reqs, ctxs, tps, block, heads, hd, exp_dev, slots, ff, share)
+    n_rem = (
+        (blocks - 1)
+        + 2
+        + 2 * (ctxs - 1)
+        + (tps - 1)
+        + (ctxs - 1)
+        + 2 * (tps - 1)
+        + 2 * tps * (reqs - 1)
+        + 4 * CHUNKS
+        + (reqs - 1)
+        + (tps - 1)
+    )
+    vmem = pl.BlockSpec(memory_space=pltpu.VMEM)
+    anywhere = pl.BlockSpec(memory_space=pl.ANY)
+    scratch = [
+        ((exp_dev, share, ff), BF16),
+        ((exp_dev, share, ff), BF16),
+        ((exp_dev, ff, share), BF16),
+        ((ctxs, hd + 8, rows), F32),
+        ((ctxs, hd + 8, rows), F32),
+        ((ctxs, block, heads * hd), BF16),
+        ((tps, block, share), F32),
+        ((tps, block, share), F32),
+        ((block, share), BF16),
+        ((block, share), F32),
+        ((ctxs, block, 128), F32),
+        ((reqs * tps, block, 128), F32),
+        ((blocks, 2 * exp_dev, 128), F32),
+        ((2 * exp_dev, tokens), F32),
+        ((reqs * tps, block, share), BF16),
+        ((exp_dev * slots, tokens), BF16),
+        ((chunk, share), BF16),
+        ((2, CHUNKS, 2, 2, quarter, ff), BF16),
+        ((2, CHUNKS, 2, quarter, ff), BF16),
+        ((2, CHUNKS, quarter, ff), BF16),
+        ((2, CHUNKS, quarter, ff), BF16),
+        ((CHUNKS, 2, 2, quarter, ff), BF16),
+        ((chunk, share), BF16),
+        ((tokens, share), F32),
+        ((reqs, tps * block, share), BF16),
+        ((reqs, tps * block, share), BF16),
+        ((tps, block, share), BF16),
+        ((tps, block, share), BF16),
+        ((block, share), BF16),
+        ((block, share), BF16),
+    ]
+    return pl.pallas_call(
+        functools.partial(layer_kernel, dims),
+        out_shape=jax.ShapeDtypeStruct((block, share), BF16),
+        in_specs=[pl.BlockSpec(memory_space=pltpu.SMEM)] + [vmem] * 9 + [anywhere] * 3,
+        out_specs=vmem,
+        scratch_shapes=[pltpu.VMEM(*s) for s in scratch]
+        + [
+            pltpu.SemaphoreType.DMA((3,)),
+            pltpu.SemaphoreType.DMA((n_rem,)),
+            pltpu.SemaphoreType.DMA((n_rem,)),
+        ],
+        compiler_params=pltpu.CompilerParams(
+            collective_id=0, has_side_effects=True, vmem_limit_bytes=63 * 1024 * 1024
+        ),
+    )(
+        cache_lengths,
+        q,
+        cache_keys[0, :, 0, :],
+        cache_values[0, :, 0, :],
+        new_keys[:, 0, :],
+        new_values[:, 0, :],
+        residual,
+        out_weight,
+        gain,
+        table,
+        w_gate,
+        w_up,
+        w_down,
+    )
 
 
 def attention_part(queries, new_keys, new_values, cache_keys, cache_values, length):
@@ -72,7 +627,7 @@
     return code.reshape(flat).T, gate_at.reshape(flat).T
 
 
-def body(
+def spread_body(
     queries,
     new_keys,
     new_values,
@@ -137,6 +692,14 @@
     return lax.ppermute(out.astype(jnp.bfloat16), ("ctx", "tp"), swap)
 
 
+def body(*args):
+    tokens = args[0].shape[0] * lax.axis_size("req")
+    slots = args[11].shape[0] * lax.axis_size("req") * lax.axis_size("ctx") * CAP
+    if tokens * slots * 2 <= FUSED_BYTES:
+        return fused_body(*args)
+    return spread_body(*args)
+
+
 def solution(mesh):
     in_specs = (
         P("req", "tp", None),

time: 256 us -> 146 us (0.57)
  blocking collectives: 111 us -> 0 us
  Pallas kernels: 0 us -> 107 us
  matrix products: 38.6 us -> 0.19 us
  waiting for transfers between devices: 36.9 us -> 0 us
  starting transfers between devices: 27.1 us -> 0 us
  local copies, waits for them, and re-layouts: 10.6 us -> 35.5 us
  between operations: 14.4 us -> 0.02 us
  other arithmetic: 14 us -> 2.2 us
    pallas_call x0 -> x1, Pallas kernels: none -> 107 us  [fused_body(): pl.pallas_call(functools.partial(layer_kernel, dims), out_shape=jax.Shape...]
    all_gather x3 -> x0, blocking collectives: 43.8 us -> none  [the longest x1 26.9 us: body(): scaled = lax.all_gather(scaled, ('req', 'tp'), tiled=True)]
    dot_general x8 -> x1, matrix products: 38.6 us -> 0.19 us  [fused_body(): rank = jnp.dot(hit.astype(BF16), later, preferred_element_type=F32)]
    psum x1 -> x0, blocking collectives: 32.9 us -> none  [body(): squares = lax.psum(squares, 'ctx')]
    unnamed x39 -> x3, local copies, waits for them, and re-layouts: 3.53 us -> 32.5 us
    all_gather x1 -> x0, waiting for transfers between devices: 22.8 us -> none  [body(): inner = lax.all_gather(inner, 'ctx', tiled=True).reshape(exp_dev, slots, -1)]
    all_to_all x3 -> x0, starting transfers between devices: 20.3 us -> none  [the longest x1 10.7 us: body(): both = lax.all_to_all(both, 'ctx', 0, 0, tiled=True)]
    all_to_all x1 -> x0, blocking collectives: 19.7 us -> none  [body(): mixed = lax.all_to_all(mixed, ('req', 'tp'), 0, 0, tiled=True)]
  transfers between devices with their start and end apart: 6 -> 0, of which waited for: 3 -> 0; matrix products, arithmetic and copies ran while one was open for 2% -> 0% of each run, Pallas kernels for 0% -> 0%
where the time goes in v2:
time: 146 us; the launch traced here: 145 us
  Pallas kernels  107 us (73%)
  local copies, waits for them, and re-layouts  35.5 us (24%)
  other arithmetic  2.2 us (2%)
    pallas_call x1, Pallas kernels, fused_body(): pl.pallas_call(functools.partial(layer_kernel, dims), out_shape=jax.Shape...  107 us
    unnamed x3, local copies, waits for them, and re-layouts  32.5 us

profile of v2, /device:TPU:1, one launch (start us, length us, event | category | flops | bytes accessed | tf_op | source)
XLA Modules:
  0.0 144.5 jit_solution(7190388415409616000)
XLA Ops:
  0.0 1.3 dynamic_slice.3
  1.3 0.7 fusion.1
  2.1 0.2 fusion
  2.3 0.7 select_reduce_fusion
  3.0 0.7 pad_maximum_fusion.1.rt_ref
  3.7 1.7 %copy.21 = bf16[4,64,4,128]{3,1,2,0:T(8,128)(2,1)} copy(bf16[4,64,4,128]{3,2,1,0:T(4,128)(2,1)} %bitcast.23) | data formatting | bytes 524288 | tf_op jit(solution)/shard_map/reshape | solution.py:473
  5.5 15.8 %copy.24.wg_hbm = bf16[32,512,352]{2,1,0:T(8,128)(2,1)} copy(bf16[32,512,352]{1,2,0:T(8,128)(2,1)} %param.25) | data formatting | bytes 23068672 | tf_op args[11]
  21.2 15.2 %copy.25.wu_hbm = bf16[32,512,352]{2,1,0:T(8,128)(2,1)} copy(bf16[32,512,352]{1,2,0:T(8,128)(2,1)} %param.26) | data formatting | bytes 23068672 | tf_op args[12]
  36.5 106.6 %shard_map.136 = bf16[64,512]{1,0:T(8,128)(2,1)} custom-call(s32[2]{0:T(128)} %len_ref.1, bf16[4,256,128]{2,1,0:T(8,128)(2,1)} %bitcast.18, bf16[2048,128]{1,0:T(8,128)(2,1)} %bitcast.19, bf16[2048,128]{1,0:T(8,128)(2,1)} %bitcast.20, bf16[256,128]{1,0:T(8,128)(2,1)} %bitcast.25, bf16[256,128]{1,0:T(8,128)(2,1)} %bitcast.26, bf16[64,512]{1,0:T(8,128)(2,1)} %res_ref.1, ...), custom_call_target="tpu_custom_call" | custom-call | tf_op jit(solution)/shard_map/pallas_call | solution.py:535
  143.1 1.5 %copy.27 = bf16[64,512]{1,0:T(8,128)(2,1)} copy(bf16[64,512]{1,0:T(8,128)(2,1)} %shard_map.136) | data formatting | bytes 131072
  (2 shorter events, 0.0 us)

commit v3 on v2

--- a/solution.py
+++ b/solution.py
@@ -40,6 +40,8 @@
     wd,
     pk_send,
     pk_recv,
+    st_send,
+    st_recv,
     att,
     part,
     part_recv,
@@ -171,26 +173,28 @@
         total = jnp.sum(old, 0, keepdims=True) + jnp.sum(new, 0, keepdims=True)
         sums = dot(cv_ref[...], old.astype(BF16), ((0,), (0,)))
         sums = sums + dot(nv_ref[...], new.astype(BF16), ((0,), (0,)))
-        pk_send[d, 0:hd, :] = sums
-        pk_send[d, hd : hd + 8, :] = jnp.where(
+        pk_send[d] = sums.astype(BF16)
+        st_send[d] = jnp.where(
             stat_at == 0, top, jnp.where(stat_at == 1, total, 0.0)
         )
         if d:
-            copy = rcopy(pk_send.at[d], pk_recv.at[d], ctx=b)
-            copy.start()
-            pk_copies.append(copy)
+            for src, dst in ((pk_send, pk_recv), (st_send, st_recv)):
+                copy = rcopy(src.at[d], dst.at[d], ctx=b)
+                copy.start()
+                pk_copies.append(copy)
     for copy in pk_copies:
         copy.wait_recv()
     pending += pk_copies
-    packs = [pk_send.at[0]] + [pk_recv.at[d] for d in range(1, ctxs)]
-    tops = [p[hd : hd + 1, :] for p in packs]
+    packs = [pk_send[0]] + [pk_recv[d] for d in range(1, ctxs)]
+    stats = [st_send[0]] + [st_recv[d] for d in range(1, ctxs)]
+    tops = [st[0:1, :] for st in stats]
     top = functools.reduce(jnp.maximum, tops)
     total = jnp.zeros((1, rows), F32)
     sums = jnp.zeros((hd, rows), F32)
-    for p, own in zip(packs, tops):
+    for p, st, own in zip(packs, stats, tops):
         factor = jnp.exp(own - top)
-        total = total + factor * p[hd + 1 : hd + 2, :]
-        sums = sums + factor * p[0:hd, :]
+        total = total + factor * st[1:2, :]
+        sums = sums + factor * p.astype(F32)
     out = jnp.transpose(sums / total)
     for h in range(heads):
         att[c, :, h * hd : (h + 1) * hd] = out[h * block : (h + 1) * block].astype(BF16)
@@ -221,14 +225,14 @@
     pending += att_copies
     width = heads * hd
     full = dot(att[...].reshape(ctxs * block, width), ow_ref[...], ((1,), (0,)))
-    part[...] = full.reshape(tps, block, share)
+    part[...] = full.reshape(tps, block, share).astype(BF16)
     part_copies = []
     for d in range(1, tps):
         to = step(t, d, tps)
         copy = rcopy(part.at[to], part_recv.at[d], tp=to)
         copy.start()
         part_copies.append(copy)
-    hid = part[t]
+    hid = part[t].astype(F32)
 
     @pl.when(c != t)
     def _():
@@ -237,7 +241,7 @@
     hid = hid + res_t[...].astype(F32)
     for d in range(1, tps):
         part_copies[d - 1].wait_recv()
-        hid = hid + part_recv[d]
+        hid = hid + part_recv[d].astype(F32)
     pending += part_copies
     hidden[...] = hid
     tok[r * tps + t] = (hid * gain_ref[...]).astype(BF16)
@@ -311,11 +315,11 @@
             at = pl.ds(pl.multiple_of((i % n_q) * rb, rb), rb)
             xs = x[pl.ds(pl.multiple_of(i * rb, rb), rb), :]
             q = i // n_q
-            gu[0, j, q // 2, q % 2, at, :] = dot(xs, wg[e], ((1,), (0,))).astype(BF16)
-            gu[1, j, q // 2, q % 2, at, :] = dot(xs, wu[e], ((1,), (0,))).astype(BF16)
+            gu[0, j, q // 2, q % 2, at, :] = dot(xs, wg[e], ((1,), (1,))).astype(BF16)
+            gu[1, j, q // 2, q % 2, at, :] = dot(xs, wu[e], ((1,), (1,))).astype(BF16)
             return carry
 
-        lax.fori_loop(0, n_sub, one, 0)
+        lax.fori_loop(0, n_sub, one, 0, unroll=min(4, n_sub))
         copy = rcopy(gu.at[:, j, :, 1 - k], r1.at[:, j], ctx=y * 2 + 1 - k)
         copy.start()
         first.append(copy)
@@ -367,7 +371,7 @@
             ys[pl.ds(rows_at, rb), :] = (down * gate).astype(BF16)
             return carry
 
-        lax.fori_loop(0, n_sub, one, 0)
+        lax.fori_loop(0, n_sub, one, 0, unroll=min(4, n_sub))
         term = dot(pick[base : base + chunk, :], ys[...], ((0,), (0,)))
         if j == 0:
             acc[...] = term
@@ -489,7 +493,7 @@
     n_rem = (
         (blocks - 1)
         + 2
-        + 2 * (ctxs - 1)
+        + 3 * (ctxs - 1)
         + (tps - 1)
         + (ctxs - 1)
         + 2 * (tps - 1)
@@ -501,14 +505,16 @@
     vmem = pl.BlockSpec(memory_space=pltpu.VMEM)
     anywhere = pl.BlockSpec(memory_space=pl.ANY)
     scratch = [
-        ((exp_dev, share, ff), BF16),
-        ((exp_dev, share, ff), BF16),
         ((exp_dev, ff, share), BF16),
-        ((ctxs, hd + 8, rows), F32),
-        ((ctxs, hd + 8, rows), F32),
+        ((exp_dev, ff, share), BF16),
+        ((exp_dev, ff, share), BF16),
+        ((ctxs, hd, rows), BF16),
+        ((ctxs, hd, rows), BF16),
+        ((ctxs, 8, rows), F32),
+        ((ctxs, 8, rows), F32),
         ((ctxs, block, heads * hd), BF16),
-        ((tps, block, share), F32),
-        ((tps, block, share), F32),
+        ((tps, block, share), BF16),
+        ((tps, block, share), BF16),
         ((block, share), BF16),
         ((block, share), F32),
         ((ctxs, block, 128), F32),
@@ -557,8 +563,8 @@
         out_weight,
         gain,
         table,
-        w_gate,
-        w_up,
+        jnp.swapaxes(w_gate, 1, 2),
+        jnp.swapaxes(w_up, 1, 2),
         w_down,
     )
 

time: 146 us -> 105 us (0.72); the launches traced: 145 us -> 105 us
  local copies, waits for them, and re-layouts: 35.5 us -> 4.51 us
  Pallas kernels: 107 us -> 98.2 us
    unnamed x3 -> x1, local copies, waits for them, and re-layouts: 32.5 us -> 1.47 us
    pallas_call x1, Pallas kernels: 107 us -> 98.2 us  [fused_body(): pl.pallas_call(functools.partial(layer_kernel, dims), out_shape=jax.Shape...]
where the time goes in v3:
time: 105 us
  Pallas kernels  98.2 us (94%)
  local copies, waits for them, and re-layouts  4.51 us (4%)
  other arithmetic  2.2 us (2%)
    pallas_call x1, Pallas kernels, fused_body(): pl.pallas_call(functools.partial(layer_kernel, dims), out_shape=jax.Shape...  98.2 us

profile of v3, /device:TPU:1, one launch (start us, length us, event | category | flops | bytes accessed | tf_op | source)
XLA Modules:
  0.0 105.1 jit_solution(2244297779511752723)
XLA Ops:
  0.0 1.3 %dynamic_slice.3 = f32[512]{0:T(512)} dynamic-slice(f32[2048]{0:T(1024)} %param.22, s32[]{:T(128)S(6)} %select_n.40), dynamic_slice_sizes={512} | dynamic-slice | bytes 4100 | tf_op jit(solution)/shard_map/dynamic_slice | solution.py:491
  1.4 0.7 fusion.1
  2.1 0.2 fusion
  2.3 0.7 select_reduce_fusion
  3.0 0.7 pad_maximum_fusion.1.rt_ref
  3.8 1.7 %copy.19 = bf16[4,64,4,128]{3,1,2,0:T(8,128)(2,1)} copy(bf16[4,64,4,128]{3,2,1,0:T(4,128)(2,1)} %bitcast.27) | data formatting | bytes 524288 | tf_op jit(solution)/shard_map/reshape | solution.py:477
  5.4 98.2 %shard_map.136 = bf16[64,512]{1,0:T(8,128)(2,1)} custom-call(s32[2]{0:T(128)} %len_ref.1, bf16[4,256,128]{2,1,0:T(8,128)(2,1)} %bitcast.22, bf16[2048,128]{1,0:T(8,128)(2,1)} %bitcast.23, bf16[2048,128]{1,0:T(8,128)(2,1)} %bitcast.24, bf16[256,128]{1,0:T(8,128)(2,1)} %bitcast.29, bf16[256,128]{1,0:T(8,128)(2,1)} %bitcast.30, bf16[64,512]{1,0:T(8,128)(2,1)} %res_ref.1, ...), custom_call_target="tpu_custom_call" | custom-call | tf_op jit(solution)/shard_map/pallas_call | solution.py:541
  103.6 1.5 %copy.23 = bf16[64,512]{1,0:T(8,128)(2,1)} copy(bf16[64,512]{1,0:T(8,128)(2,1)} %shard_map.136) | data formatting | bytes 131072
  (2 shorter events, 0.0 us)
